TPU v7x, 128 devices: a whole 4x4x4 slice. The times are simulated.
128 devices in a mesh: samp: 32 (over y, x, core), slab: 4 (over z).
Axes of the slice: x: 4, y: 4, z: 4, core: 2. Of those that a mesh axis runs over, the one named last changes fastest.
Arguments:
- ld_blocks: bfloat16 [4, 64, 768, 768], P('slab', 'samp'), may hold values from -1 to 1, as said below
- marginal: float32 [4, 49152], P('slab', 'samp'), may hold values from -1.8 to 1.8
- normals: float32 [2, 4, 49152], P(None, 'slab', 'samp'), may hold values from -6 to 6
- block_len: int32 [64], P('samp'), may hold values from 1 to 768, 36864 in all
- scale_start: float32 [49152], P('samp'), may hold values from 0.2 to 5
- ancestry_weight: float32 [4], replicated, may hold values from 4 to 64
- dosage: bfloat16 [4096, 49152], P('samp', 'slab'), may hold values from 0 to 2
Outputs:
- effects: float32 [4, 49152], P('slab', 'samp')
- shrink: float32 [49152], P('samp')
- scores: float32 [4096, 4], P('samp', 'slab')
Inputs may be any that keep to these rules, and one draw needn't show every extreme that they name: `block_len`: the block lengths sum to 36864; the longest is exactly 768. `ld_blocks`: every block is symmetric with unit diagonal, and it and each of its leading principal submatrices is positive definite.
All inputs are finite; a program needn't handle non-finite values.
Results may differ from a plain program's by a relative error of at most 0.0031.
Values may be sent and summed in bfloat16 or wider, within the bound.
A program may use at most 128 MiB of HBM per device.

v0:
```python
import jax
import jax.numpy as jnp
from jax import lax
from jax.sharding import PartitionSpec as P

SWEEPS = 2
shape_total = 1.5
global_shrink = 0.01


def mean_rounded(stacked):
    total = stacked[:, 0]
    total = total + stacked[:, 1]
    return (total / stacked.shape[1]).astype(jnp.bfloat16)


def score_terms(columns, weights):
    product = lax.dot_general(
        columns, weights, (((1,), (1,)), ((), ())), preferred_element_type=jnp.float32
    )
    return (product, jnp.sum(weights.astype(jnp.float32), axis=1))


def per_device(ld_blocks, marginal, normals, block_len, scale_start, ancestry_weight, dosage):
    slot_count = ld_blocks.shape[1]
    block_size = ld_blocks.shape[2]
    ancestries = ancestry_weight.shape[0]
    own_index = lax.axis_index("slab")
    weight = lax.dynamic_index_in_dim(ancestry_weight, own_index, 0, keepdims=False)
    position = jnp.arange(block_size, dtype=jnp.int32)
    live_rows = (position[None, :] < block_len[:, None]).astype(jnp.float32)
    correlation = ld_blocks[0].astype(jnp.float32) * (live_rows[:, :, None] * live_rows[:, None, :])
    identity = jnp.eye(block_size, dtype=jnp.float32)
    targets = marginal[0].reshape(slot_count, block_size) * live_rows
    shrink = scale_start.reshape(slot_count, block_size)
    shrink_rate = shape_total / (shrink + global_shrink)
    variance = jnp.ones((), jnp.float32)
    local_live = jnp.sum(live_rows)
    live_total = local_live
    drawn = []
    for sweep_index in range(SWEEPS):
        inverse = 1.0 / shrink
        system = (
            correlation
            + identity[None, :, :] * (live_rows * inverse + (1.0 - live_rows))[:, None, :]
        )
        factor = jnp.linalg.cholesky(system)
        forward = lax.linalg.triangular_solve(
            factor, targets[:, :, None], left_side=True, lower=True
        )[:, :, 0]
        noise_level = jnp.sqrt(variance / weight)
        forward = (
            forward
            + noise_level * normals[sweep_index, 0].reshape(slot_count, block_size) * live_rows
        )
        effect = lax.linalg.triangular_solve(
            factor, forward[:, :, None], left_side=True, lower=True, transpose_a=True
        )[:, :, 0]
        fitted = jnp.einsum("sij,sj->si", correlation, effect, precision=lax.Precision.HIGHEST)
        misfit = targets - fitted
        stat_row = jnp.stack(
            [jnp.sum(misfit * misfit), jnp.sum(effect * effect * inverse * live_rows), local_live]
        )
        totals = lax.psum(stat_row, "samp")
        variance = (totals[0] + totals[1] + 1.0) / (totals[2] + 1.0)
        pooled = lax.psum(weight * effect * effect / variance, "slab")
        live_total = totals[2]
        shrink = (pooled + 1.0) / (2.0 + jnp.sqrt(4.0 + 2.0 * shrink_rate * (pooled + 1.0)))
        shrink_rate = shape_total / (shrink + global_shrink)
        drawn.append(effect.reshape(1, slot_count * block_size))
    total = drawn[0]
    sweep_index = 1
    total = total + drawn[sweep_index]
    effects = total / SWEEPS
    stacked = jnp.concatenate(drawn, axis=0)
    slab_count = lax.axis_size("slab")
    samp_count = lax.axis_size("samp")
    quarter = slot_count * block_size // slab_count
    spread = lax.all_gather(stacked, "samp", axis=1, tiled=True)
    layout = spread.reshape(1, SWEEPS, samp_count, slab_count, quarter)
    received = lax.all_to_all(layout, "slab", split_axis=3, concat_axis=0, tiled=True)
    weights = mean_rounded(received.reshape(ancestries, SWEEPS, samp_count * quarter))
    products, column_sums = score_terms(dosage, weights)
    partial_value = products - column_sums[None, :]
    scores = lax.psum_scatter(partial_value, "slab", scatter_dimension=1, tiled=True) / jnp.sqrt(
        live_total
    )
    return (effects, shrink.reshape(slot_count * block_size), scores)


def solution(mesh):
    return jax.shard_map(
        per_device,
        mesh=mesh,
        in_specs=(
            P("slab", "samp", None, None),
            P("slab", "samp"),
            P(None, "slab", "samp"),
            P("samp"),
            P("samp"),
            P(),
            P("samp", "slab"),
        ),
        out_specs=(P("slab", "samp"), P("samp"), P("samp", "slab")),
        check_vma=False,
    )
```

profile of v0, /device:TPU:0, one launch (start us, length us, event | category | flops | bytes accessed | tf_op | source)
XLA Modules:
  0.0 1182.4 jit_solution(14147899627568268930)
XLA Ops:
  6.4 4.3 copy.120
  11.4 4.2 multiply_add_fusion.1
  15.7 6.2 copy.121
  21.8 4.4 fusion.1
  28.3 23.5 %custom-call.57 = f32[2,128,128]{2,1,0:T(8,128)S(1)} custom-call(f32[2,128,128]{2,1,0:T(8,128)S(1)} %cholesky.662), custom_call_target="Cholesky" | custom-call | tf_op jit(solution)/shard_map/jit(cholesky)/cholesky | solution.py:47
  51.8 19.7 %custom-call.58 = f32[2,1,128,128]{2,3,1,0:T(8,128)S(1)} custom-call(f32[2,1,128,128]{3,2,1,0:T(8,128)S(1)} %select_bitcast_fusion.9), custom_call_target="InvertDiagBlocksLowerTriangular" | custom-call | tf_op jit(solution)/shard_map/jit(cholesky)/cholesky | solution.py:47
  79.4 24.0 %custom-call.59 = f32[2,128,128]{2,1,0:T(8,128)S(1)} custom-call(f32[2,128,128]{2,1,0:T(8,128)S(1)} %cholesky.666), custom_call_target="Cholesky" | custom-call | tf_op jit(solution)/shard_map/jit(cholesky)/cholesky | solution.py:47
  104.2 19.7 %custom-call.60 = f32[2,1,128,128]{2,3,1,0:T(8,128)S(1)} custom-call(f32[2,1,128,128]{3,2,1,0:T(8,128)S(1)} %get-tuple-element.95), custom_call_target="InvertDiagBlocksLowerTriangular" | custom-call | tf_op jit(solution)/shard_map/jit(cholesky)/cholesky | solution.py:47
  129.7 23.5 %custom-call.61 = f32[2,128,128]{2,1,0:T(8,128)S(1)} custom-call(f32[2,128,128]{2,1,0:T(8,128)S(1)} %cholesky.671), custom_call_target="Cholesky" | custom-call | tf_op jit(solution)/shard_map/jit(cholesky)/cholesky | solution.py:47
  153.9 20.6 %custom-call.62 = f32[2,1,128,128]{2,3,1,0:T(8,128)S(1)} custom-call(f32[2,1,128,128]{3,2,1,0:T(8,128)} %get-tuple-element.93), custom_call_target="InvertDiagBlocksLowerTriangular" | custom-call | tf_op jit(solution)/shard_map/jit(cholesky)/cholesky | solution.py:47
  180.3 24.9 %custom-call.63 = f32[2,128,128]{2,1,0:T(8,128)} custom-call(f32[2,128,128]{2,1,0:T(8,128)} %cholesky.676), custom_call_target="Cholesky" | custom-call | tf_op jit(solution)/shard_map/jit(cholesky)/cholesky | solution.py:47
  206.8 21.1 %custom-call.64 = f32[2,1,128,128]{2,3,1,0:T(8,128)} custom-call(f32[2,1,128,128]{3,2,1,0:T(8,128)} %get-tuple-element.91), custom_call_target="InvertDiagBlocksLowerTriangular" | custom-call | tf_op jit(solution)/shard_map/jit(cholesky)/cholesky | solution.py:47
  233.1 24.5 %custom-call.65 = f32[2,128,128]{2,1,0:T(8,128)S(1)} custom-call(f32[2,128,128]{2,1,0:T(8,128)} %cholesky.681), custom_call_target="Cholesky" | custom-call | tf_op jit(solution)/shard_map/jit(cholesky)/cholesky | solution.py:47
  258.3 21.1 %custom-call.66 = f32[2,1,128,128]{2,3,1,0:T(8,128)} custom-call(f32[2,1,128,128]{3,2,1,0:T(8,128)} %get-tuple-element.89), custom_call_target="InvertDiagBlocksLowerTriangular" | custom-call | tf_op jit(solution)/shard_map/jit(cholesky)/cholesky | solution.py:47
  283.4 23.5 %custom-call.67 = f32[2,128,128]{2,1,0:T(8,128)S(1)} custom-call(f32[2,128,128]{2,1,0:T(8,128)S(1)} %convolution_subtract_fusion.9), custom_call_target="Cholesky" | custom-call | tf_op jit(solution)/shard_map/jit(cholesky)/cholesky | solution.py:47
  309.2 5.3 select_select_fusion.1
  315.6 22.0 %while.8 = (s32[]{:T(128)}, f32[2,768,768]{2,1,0:T(8,128)}, s32[6,2]{0,1:T(2,128)S(1)}, f32[6,2,128,128]{3,2,0,1:T(8,128)}, s32[]{:T(128)}) while((s32[]{:T(128)}, f32[2,768,768]{2,1,0:T(8,128)}, s32[6,2]{0,1:T(2,128)S(1)}, f32[6,2,128,128]{3,2,0,1:T(8,128)}, s32[]{:T(128)}) %tuple.92), condition=%wide.while_cond.1, body=%wide.while_body.1.sunk | while | flops 2 | bytes 263777 | solution.py:56
  316.2 3.0 bitcast_dynamic-update-slice_fusion.4
  319.9 3.0 bitcast_dynamic-update-slice_fusion.4
  323.6 3.0 bitcast_dynamic-update-slice_fusion.4
  327.3 3.0 bitcast_dynamic-update-slice_fusion.4
  330.9 3.0 bitcast_dynamic-update-slice_fusion.4
  337.6 119.7 %custom-call.69 = f32[2,6,128,128]{2,3,1,0:T(8,128)} custom-call(f32[2,6,128,128]{3,2,1,0:T(8,128)} %bitcast.493), custom_call_target="InvertDiagBlocksLowerTriangular" | custom-call | tf_op jit(solution)/shard_map/triangular_solve/custom-call.12 | solution.py:56
  487.8 4.6 fusion.3
  495.2 67.4 %psum.28 = f32[3]{0:T(128)S(1)} all-reduce(f32[3]{0:T(128)S(1)} %maximum_maximum_fusion), channel_id=1, replica_groups=mesh['samp'=32,'slab'=4] {'samp'}, use_global_device_ids=true, to_apply=%region_15.19 | all-reduce | flops 3 | bytes 24 | tf_op jit(solution)/shard_map/psum | solution.py:64
  567.2 11.9 %psum.29 = f32[2,768]{1,0:T(2,128)S(1)} all-reduce(f32[2,768]{1,0:T(2,128)S(1)} %fusion.118), channel_id=1, replica_groups=mesh['samp'=32,'slab'=4] {'slab'}, use_global_device_ids=true, to_apply=%region_16.20 | all-reduce | flops 1536 | bytes 12288 | tf_op jit(solution)/shard_map/psum | solution.py:66
  579.8 4.5 multiply_add_fusion
  584.3 6.1 copy.134
  590.3 4.4 fusion
  596.8 23.5 %custom-call.70 = f32[2,128,128]{2,1,0:T(8,128)S(1)} custom-call(f32[2,128,128]{2,1,0:T(8,128)S(1)} %cholesky.685), custom_call_target="Cholesky" | custom-call | tf_op jit(solution)/shard_map/jit(cholesky)/cholesky | solution.py:47
  622.8 19.7 %custom-call.71 = f32[2,1,128,128]{2,3,1,0:T(8,128)S(1)} custom-call(f32[2,1,128,128]{3,2,1,0:T(8,128)S(1)} %select_bitcast_fusion.4), custom_call_target="InvertDiagBlocksLowerTriangular" | custom-call | tf_op jit(solution)/shard_map/jit(cholesky)/cholesky | solution.py:47
  647.9 23.7 %custom-call.72 = f32[2,128,128]{2,1,0:T(8,128)S(1)} custom-call(f32[2,128,128]{2,1,0:T(8,128)S(1)} %cholesky.689), custom_call_target="Cholesky" | custom-call | tf_op jit(solution)/shard_map/jit(cholesky)/cholesky | solution.py:47
  672.3 19.7 %custom-call.73 = f32[2,1,128,128]{2,3,1,0:T(8,128)S(1)} custom-call(f32[2,1,128,128]{3,2,1,0:T(8,128)S(1)} %get-tuple-element.86), custom_call_target="InvertDiagBlocksLowerTriangular" | custom-call | tf_op jit(solution)/shard_map/jit(cholesky)/cholesky | solution.py:47
  697.8 23.5 %custom-call.74 = f32[2,128,128]{2,1,0:T(8,128)S(1)} custom-call(f32[2,128,128]{2,1,0:T(8,128)S(1)} %cholesky.694), custom_call_target="Cholesky" | custom-call | tf_op jit(solution)/shard_map/jit(cholesky)/cholesky | solution.py:47
  722.1 20.9 %custom-call.75 = f32[2,1,128,128]{2,3,1,0:T(8,128)S(1)} custom-call(f32[2,1,128,128]{3,2,1,0:T(8,128)} %get-tuple-element.84), custom_call_target="InvertDiagBlocksLowerTriangular" | custom-call | tf_op jit(solution)/shard_map/jit(cholesky)/cholesky | solution.py:47
  748.6 24.9 %custom-call.76 = f32[2,128,128]{2,1,0:T(8,128)} custom-call(f32[2,128,128]{2,1,0:T(8,128)} %cholesky.699), custom_call_target="Cholesky" | custom-call | tf_op jit(solution)/shard_map/jit(cholesky)/cholesky | solution.py:47
  775.2 21.1 %custom-call.77 = f32[2,1,128,128]{2,3,1,0:T(8,128)} custom-call(f32[2,1,128,128]{3,2,1,0:T(8,128)} %get-tuple-element.82), custom_call_target="InvertDiagBlocksLowerTriangular" | custom-call | tf_op jit(solution)/shard_map/jit(cholesky)/cholesky | solution.py:47
  801.4 24.4 %custom-call.78 = f32[2,128,128]{2,1,0:T(8,128)S(1)} custom-call(f32[2,128,128]{2,1,0:T(8,128)} %cholesky.704), custom_call_target="Cholesky" | custom-call | tf_op jit(solution)/shard_map/jit(cholesky)/cholesky | solution.py:47
  826.6 21.1 %custom-call.79 = f32[2,1,128,128]{2,3,1,0:T(8,128)} custom-call(f32[2,1,128,128]{3,2,1,0:T(8,128)} %get-tuple-element.80), custom_call_target="InvertDiagBlocksLowerTriangular" | custom-call | tf_op jit(solution)/shard_map/jit(cholesky)/cholesky | solution.py:47
  851.7 23.5 %custom-call.80 = f32[2,128,128]{2,1,0:T(8,128)S(1)} custom-call(f32[2,128,128]{2,1,0:T(8,128)S(1)} %convolution_subtract_fusion.8), custom_call_target="Cholesky" | custom-call | tf_op jit(solution)/shard_map/jit(cholesky)/cholesky | solution.py:47
  877.8 5.3 select_select_fusion
  884.1 21.5 %while.9 = (s32[]{:T(128)}, f32[2,768,768]{2,1,0:T(8,128)}, s32[6,2]{0,1:T(2,128)S(1)}, f32[6,2,128,128]{3,2,0,1:T(8,128)}, s32[]{:T(128)}) while((s32[]{:T(128)}, f32[2,768,768]{2,1,0:T(8,128)}, s32[6,2]{0,1:T(2,128)S(1)}, f32[6,2,128,128]{3,2,0,1:T(8,128)}, s32[]{:T(128)}) %tuple.98), condition=%wide.while_cond.1.clone, body=%wide.while_body.1.clone.sunk | while | flops 2 | bytes 263777 | solution.py:56
  905.7 119.5 %custom-call.82 = f32[2,6,128,128]{2,3,1,0:T(8,128)} custom-call(f32[2,6,128,128]{3,2,1,0:T(8,128)} %bitcast.492), custom_call_target="InvertDiagBlocksLowerTriangular" | custom-call | tf_op jit(solution)/shard_map/triangular_solve/custom-call.12 | solution.py:56
  1054.7 22.0 %all_gather.3 = f32[2,49152]{1,0:T(2,128)S(1)} all-gather(f32[2,1536]{1,0:T(2,128)S(1)} %pad_maximum_fusion), channel_id=1, replica_groups=mesh['samp'=32,'slab'=4] {'samp'}, dimensions={1}, use_global_device_ids=true | all-gather | bytes 405504 | tf_op jit(solution)/shard_map/all_gather | solution.py:79
  1079.6 3.7 all-to-all-start
  1083.3 4.6 fusion.2
  1093.2 65.9 %psum.30 = f32[3]{0:T(128)} all-reduce(f32[3]{0:T(128)} %maximum_maximum_fusion.1), channel_id=1, replica_groups=mesh['samp'=32,'slab'=4] {'samp'}, use_global_device_ids=true, to_apply=%region_19.23 | all-reduce | flops 3 | bytes 24 | tf_op jit(solution)/shard_map/psum | solution.py:64
  1169.2 10.9 all-reduce.2
  (333 shorter events, 192.8 us)
Async XLA Ops:
  0.6 1167.7 %copy-start = (bf16[128,12288]{1,0:T(8,128)(2,1)S(1)}, bf16[128,12288]{1,0:T(8,128)(2,1)}, u32[]{:S(2)}) copy-start(bf16[128,12288]{1,0:T(8,128)(2,1)} %param.18) | copy-start | bytes 9437188
  0.6 10.0 copy-start.32
  0.7 10.1 copy-start.40
  10.7 11.1 copy-start.13
  11.4 4.3 copy-start.24
  26.2 2.1 copy-start.2
  51.8 27.6 %copy-start.7 = (f32[2,128,128]{2,1,0:T(8,128)}, f32[2,128,128]{2,1,0:T(8,128)S(1)}, u32[]{:S(2)}) copy-start(f32[2,128,128]{2,1,0:T(8,128)S(1)} %custom-call.57) | copy-start | bytes 393220
  78.6 0.8 copy-start.3
  103.4 71.1 %copy-start.9 = (f32[2,128,128]{2,1,0:T(8,128)}, f32[2,128,128]{2,1,0:T(8,128)S(1)}, u32[]{:S(2)}) copy-start(f32[2,128,128]{2,1,0:T(8,128)S(1)} %custom-call.59) | copy-start | bytes 393220
  128.9 0.8 copy-start.5
  153.1 21.4 %copy-start.11 = (f32[2,128,128]{2,1,0:T(8,128)}, f32[2,128,128]{2,1,0:T(8,128)S(1)}, u32[]{:S(2)}) copy-start(f32[2,128,128]{2,1,0:T(8,128)S(1)} %custom-call.61) | copy-start | bytes 393220
  309.2 5.3 copy-start.42
  309.2 148.1 %copy-start.33 = (s32[2]{0:T(128)S(1)}, s32[2]{0:T(128)}, u32[]{:S(2)}) copy-start(s32[2]{0:T(128)} %param.15) | copy-start | bytes 28
  309.2 148.1 %copy-start.36 = (f32[2,768,1]{1,0,2:T(2,128)S(1)}, f32[2,768,1]{1,0,2:T(2,128)}, u32[]{:S(2)}) copy-start(f32[2,768,1]{1,0,2:T(2,128)} %reshape_squeeze.13) | copy-start | bytes 18436
  314.5 157.3 %copy-start.41 = (f32[4]{0:T(128)S(1)}, f32[4]{0:T(128)}, u32[]{:S(2)}) copy-start(f32[4]{0:T(128)} %param.17) | copy-start | bytes 52
  314.5 158.8 %copy-start.37 = (f32[2,1,1536]{2,1,0:T(1,128)S(1)}, f32[2,1,1536]{2,1,0:T(1,128)}, u32[]{:S(2)}) copy-start(f32[2,1,1536]{2,1,0:T(1,128)} %param.14) | copy-start | bytes 36868
  314.5 173.2 %copy-start.14 = (f32[2,768]{1,0:T(2,128)S(1)}, f32[2,768]{1,0:T(2,128)}, u32[]{:S(2)}) copy-start(f32[2,768]{1,0:T(2,128)} %copy-done.13) | copy-start | bytes 18436
  337.6 154.8 %copy-start.16 = (s32[6,2]{0,1:T(2,128)}, s32[6,2]{0,1:T(2,128)S(1)}, u32[]{:S(2)}) copy-start(s32[6,2]{0,1:T(2,128)S(1)} %get-tuple-element.228) | copy-start | bytes 148
  457.4 30.3 %copy-start.29 = (f32[2,768,1]{1,0,2:T(2,128)}, f32[2,768,1]{1,0,2:T(2,128)S(1)}, u32[]{:S(2)}) copy-start(f32[2,768,1]{1,0,2:T(2,128)S(1)} %fusion.130) | copy-start | bytes 18436
  457.4 15.9 %copy-start.38 = (f32[2,128,1]{1,0,2:T(2,128)}, f32[2,128,1]{1,0,2:T(2,128)S(1)}, u32[]{:S(2)}) copy-start(f32[2,128,1]{1,0,2:T(2,128)S(1)} %slice.368) | copy-start | bytes 3076
  463.4 29.1 %copy-start.25 = (f32[2,768]{1,0:T(2,128)S(1)}, f32[2,768]{1,0:T(2,128)}, u32[]{:S(2)}) copy-start(f32[2,768]{1,0:T(2,128)} %copy-done.24) | copy-start | bytes 18436
  463.4 29.1 %copy-start.28 = (f32[2,768]{1,0:T(2,128)S(1)}, f32[2,768]{1,0:T(2,128)}, u32[]{:S(2)}) copy-start(f32[2,768]{1,0:T(2,128)} %reshape_squeeze.15) | copy-start | bytes 18436
  463.4 115.8 %copy-start.31 = (f32[1536]{0:T(1024)S(1)}, f32[1536]{0:T(1024)}, u32[]{:S(2)}) copy-start(f32[1536]{0:T(1024)} %get-tuple-element.97) | copy-start | bytes 18436
  487.8 96.5 %copy-start.18 = (f32[2,768,1]{1,0,2:T(2,128)}, f32[2,768,1]{1,0,2:T(2,128)S(1)}, u32[]{:S(2)}) copy-start(f32[2,768,1]{1,0,2:T(2,128)S(1)} %constant_dynamic-update-slice_fusion.16) | copy-start | bytes 18436
  579.1 5.1 copy-start.22
  579.2 5.1 copy-start.20
  594.7 2.1 copy-start.1
  620.3 27.6 %copy-start.8 = (f32[2,128,128]{2,1,0:T(8,128)}, f32[2,128,128]{2,1,0:T(8,128)S(1)}, u32[]{:S(2)}) copy-start(f32[2,128,128]{2,1,0:T(8,128)S(1)} %custom-call.70) | copy-start | bytes 393220
  647.1 0.8 copy-start.4
  671.6 71.3 %copy-start.10 = (f32[2,128,128]{2,1,0:T(8,128)}, f32[2,128,128]{2,1,0:T(8,128)S(1)}, u32[]{:S(2)}) copy-start(f32[2,128,128]{2,1,0:T(8,128)S(1)} %custom-call.72) | copy-start | bytes 393220
  697.0 0.8 copy-start.6
  721.3 21.6 %copy-start.12 = (f32[2,128,128]{2,1,0:T(8,128)}, f32[2,128,128]{2,1,0:T(8,128)S(1)}, u32[]{:S(2)}) copy-start(f32[2,128,128]{2,1,0:T(8,128)S(1)} %custom-call.74) | copy-start | bytes 393220
  877.8 6.4 copy-start.17
  877.8 147.4 %copy-start.39 = (f32[2,128,1]{1,0,2:T(2,128)S(1)}, f32[2,128,1]{1,0,2:T(2,128)}, u32[]{:S(2)}) copy-start(f32[2,128,1]{1,0,2:T(2,128)} %copy-done.38) | copy-start | bytes 3076
  877.8 149.7 %copy-start.30 = (f32[2,768,1]{1,0,2:T(2,128)S(1)}, f32[2,768,1]{1,0,2:T(2,128)}, u32[]{:S(2)}) copy-start(f32[2,768,1]{1,0,2:T(2,128)} %copy-done.29) | copy-start | bytes 18436
  883.1 156.5 %copy-start.34 = (s32[2]{0:T(128)S(1)}, s32[2]{0:T(128)}, u32[]{:S(2)}) copy-start(s32[2]{0:T(128)} %param.15) | copy-start | bytes 28
  883.1 156.5 %copy-start.35 = (f32[2,768,1]{1,0,2:T(2,128)S(1)}, f32[2,768,1]{1,0,2:T(2,128)}, u32[]{:S(2)}) copy-start(f32[2,768,1]{1,0,2:T(2,128)} %mul.175) | copy-start | bytes 18436
  883.1 170.9 %copy-start.19 = (f32[2,768,1]{1,0,2:T(2,128)S(1)}, f32[2,768,1]{1,0,2:T(2,128)}, u32[]{:S(2)}) copy-start(f32[2,768,1]{1,0,2:T(2,128)} %copy-done.18) | copy-start | bytes 18436
  884.1 199.2 %copy-start.15 = (f32[2,768]{1,0:T(2,128)S(1)}, f32[2,768]{1,0:T(2,128)}, u32[]{:S(2)}) copy-start(f32[2,768]{1,0:T(2,128)} %copy-done.13) | copy-start | bytes 18436
  1054.0 0.6 copy-start.26
  1054.1 0.6 copy-start.27
  1079.6 86.1 %all-to-all-start = ((f32[1,2,32,4,384]{4,2,1,0,3:T(8,128)}), f32[1,2,32,4,384]{4,2,1,0,3:T(8,128)S(1)}, u32[]{:S(2)}, u32[]{:S(2)}) async-start(f32[1,2,32,4,384]{4,2,1,0,3:T(8,128)} %copy.147), calls=%async_computation | async-start | bytes 786432 | tf_op jit(solution)/shard_map/all_to_all | solution.py:81
  1088.0 92.1 %copy-start.21 = (f32[2,768]{1,0:T(2,128)S(1)}, f32[2,768]{1,0:T(2,128)}, u32[]{:S(2)}) copy-start(f32[2,768]{1,0:T(2,128)} %copy-done.20) | copy-start | bytes 18436
  1165.6 14.5 %copy-start.23 = (f32[2,768]{1,0:T(2,128)S(1)}, f32[2,768]{1,0:T(2,128)}, u32[]{:S(2)}) copy-start(f32[2,768]{1,0:T(2,128)} %copy-done.22) | copy-start | bytes 18436
where the time goes:
time: 1190 us; the launch traced here: 1180 us
  other arithmetic  791 us (66%)
  blocking collectives  178 us (15%)
  matrix products  113 us (9%)
  local copies, waits for them, and re-layouts  88.5 us (7%)
    another operation x47, other arithmetic, per_device(): factor = jnp.linalg.cholesky(system)  505 us
    another operation x22, other arithmetic, per_device(): lax.linalg.triangular_solve(factor, forward[:, :, None], left_side=True,...  251 us
    psum x2, blocking collectives, per_device(): totals = lax.psum(stat_row, 'samp')  133 us
    another operation x20, matrix products, per_device(): factor = jnp.linalg.cholesky(system)  46.3 us
    another operation x45, local copies, waits for them, and re-layouts, per_device(): lax.linalg.triangular_solve(factor, forward[:, :, None], left_side=True,...  45.6 us
    another operation x22, matrix products, per_device(): lax.linalg.triangular_solve(factor, targets[:, :, None], left_side=True,...  28.6 us
    another operation x22, matrix products, per_device(): lax.linalg.triangular_solve(factor, forward[:, :, None], left_side=True,...  28.2 us
  transfers between devices with their start and end apart: 1, of which 0 were waited for; matrix products, arithmetic and copies ran while one was open for 1% of the time, Pallas kernels for 0%

commit v1 on v0

--- a/solution.py
+++ b/solution.py
@@ -61,7 +61,10 @@
         stat_row = jnp.stack(
             [jnp.sum(misfit * misfit), jnp.sum(effect * effect * inverse * live_rows), local_live]
         )
-        totals = lax.psum(stat_row, "samp")
+        size, totals = (lax.axis_size("samp"), stat_row)
+        for reach in [1 << k for k in range(size.bit_length() - 1)]:
+            route = [(i, i ^ reach) for i in range(size)]
+            totals = totals + lax.ppermute(totals, "samp", route)
         variance = (totals[0] + totals[1] + 1.0) / (totals[2] + 1.0)
         pooled = lax.psum(weight * effect * effect / variance, "slab")
         live_total = totals[2]

time: 1190 us -> 1100 us (0.924)
  blocking collectives: 178 us -> 48.3 us
  waiting for transfers between devices: 0.01 us -> 18.2 us
  starting transfers between devices: 3.71 us -> 21.3 us
    psum x2 -> x0, blocking collectives: 133 us -> none  [per_device(): totals = lax.psum(stat_row, 'samp')]
    ppermute x0 -> x10, waiting for transfers between devices: none -> 18.2 us  [per_device(): totals = totals + lax.ppermute(totals, 'samp', route)]
    ppermute x0 -> x10, starting transfers between devices: none -> 17.7 us  [per_device(): totals = totals + lax.ppermute(totals, 'samp', route)]
  transfers between devices with their start and end apart: 1 -> 11, of which waited for: 0 -> 9; matrix products, arithmetic and copies ran while one was open for 1% -> 1% of each run, Pallas kernels for 0% -> 0%
where the time goes in v1:
time: 1100 us; the launch traced here: 1090 us
  other arithmetic  797 us (72%)
  matrix products  112 us (10%)
  local copies, waits for them, and re-layouts  87 us (8%)
  blocking collectives  48.3 us (4%)
  starting transfers between devices  21.3 us (2%)
  waiting for transfers between devices  18.2 us (2%)
    another operation x47, other arithmetic, per_device(): factor = jnp.linalg.cholesky(system)  505 us
    another operation x22, other arithmetic, per_device(): lax.linalg.triangular_solve(factor, forward[:, :, None], left_side=True,...  251 us
    another operation x20, matrix products, per_device(): factor = jnp.linalg.cholesky(system)  46.3 us
    another operation x45, local copies, waits for them, and re-layouts, per_device(): lax.linalg.triangular_solve(factor, forward[:, :, None], left_side=True,...  45.5 us
    another operation x22, matrix products, per_device(): lax.linalg.triangular_solve(factor, targets[:, :, None], left_side=True,...  28.8 us
    another operation x22, matrix products, per_device(): lax.linalg.triangular_solve(factor, forward[:, :, None], left_side=True,...  28.2 us
    all_gather x1, blocking collectives, per_device(): spread = lax.all_gather(stacked, 'samp', axis=1, tiled=True)  25.2 us
    psum x2, blocking collectives, per_device(): pooled = lax.psum(weight * effect * effect / variance, 'slab')  23.1 us
  transfers between devices with their start and end apart: 11, of which 9 were waited for; matrix products, arithmetic and copies ran while one was open for 1% of the time, Pallas kernels for 0%

profile of v1, /device:TPU:0, one launch (start us, length us, event | category | flops | bytes accessed | tf_op | source)
XLA Modules:
  0.0 1092.7 jit_solution(10772897058031126667)
XLA Ops:
  6.4 4.3 copy.120
  11.4 4.2 multiply_add_fusion.1
  15.7 6.2 copy.121
  21.8 4.4 fusion.1
  28.3 23.5 %custom-call.57 = f32[2,128,128]{2,1,0:T(8,128)S(1)} custom-call(f32[2,128,128]{2,1,0:T(8,128)S(1)} %cholesky.662), custom_call_target="Cholesky" | custom-call | tf_op jit(solution)/shard_map/jit(cholesky)/cholesky | solution.py:47
  51.8 19.7 %custom-call.58 = f32[2,1,128,128]{2,3,1,0:T(8,128)S(1)} custom-call(f32[2,1,128,128]{3,2,1,0:T(8,128)S(1)} %select_bitcast_fusion.9), custom_call_target="InvertDiagBlocksLowerTriangular" | custom-call | tf_op jit(solution)/shard_map/jit(cholesky)/cholesky | solution.py:47
  79.4 23.6 %custom-call.59 = f32[2,128,128]{2,1,0:T(8,128)S(1)} custom-call(f32[2,128,128]{2,1,0:T(8,128)S(1)} %cholesky.666), custom_call_target="Cholesky" | custom-call | tf_op jit(solution)/shard_map/jit(cholesky)/cholesky | solution.py:47
  103.8 19.7 %custom-call.60 = f32[2,1,128,128]{2,3,1,0:T(8,128)S(1)} custom-call(f32[2,1,128,128]{3,2,1,0:T(8,128)S(1)} %get-tuple-element.95), custom_call_target="InvertDiagBlocksLowerTriangular" | custom-call | tf_op jit(solution)/shard_map/jit(cholesky)/cholesky | solution.py:47
  129.3 23.5 %custom-call.61 = f32[2,128,128]{2,1,0:T(8,128)S(1)} custom-call(f32[2,128,128]{2,1,0:T(8,128)S(1)} %cholesky.671), custom_call_target="Cholesky" | custom-call | tf_op jit(solution)/shard_map/jit(cholesky)/cholesky | solution.py:47
  153.6 20.7 %custom-call.62 = f32[2,1,128,128]{2,3,1,0:T(8,128)S(1)} custom-call(f32[2,1,128,128]{3,2,1,0:T(8,128)} %get-tuple-element.93), custom_call_target="InvertDiagBlocksLowerTriangular" | custom-call | tf_op jit(solution)/shard_map/jit(cholesky)/cholesky | solution.py:47
  179.9 24.9 %custom-call.63 = f32[2,128,128]{2,1,0:T(8,128)} custom-call(f32[2,128,128]{2,1,0:T(8,128)} %cholesky.676), custom_call_target="Cholesky" | custom-call | tf_op jit(solution)/shard_map/jit(cholesky)/cholesky | solution.py:47
  206.5 21.1 %custom-call.64 = f32[2,1,128,128]{2,3,1,0:T(8,128)} custom-call(f32[2,1,128,128]{3,2,1,0:T(8,128)} %get-tuple-element.91), custom_call_target="InvertDiagBlocksLowerTriangular" | custom-call | tf_op jit(solution)/shard_map/jit(cholesky)/cholesky | solution.py:47
  232.8 24.6 %custom-call.65 = f32[2,128,128]{2,1,0:T(8,128)S(1)} custom-call(f32[2,128,128]{2,1,0:T(8,128)} %cholesky.681), custom_call_target="Cholesky" | custom-call | tf_op jit(solution)/shard_map/jit(cholesky)/cholesky | solution.py:47
  258.2 21.1 %custom-call.66 = f32[2,1,128,128]{2,3,1,0:T(8,128)} custom-call(f32[2,1,128,128]{3,2,1,0:T(8,128)} %get-tuple-element.89), custom_call_target="InvertDiagBlocksLowerTriangular" | custom-call | tf_op jit(solution)/shard_map/jit(cholesky)/cholesky | solution.py:47
  283.3 23.5 %custom-call.67 = f32[2,128,128]{2,1,0:T(8,128)S(1)} custom-call(f32[2,128,128]{2,1,0:T(8,128)S(1)} %convolution_subtract_fusion.9), custom_call_target="Cholesky" | custom-call | tf_op jit(solution)/shard_map/jit(cholesky)/cholesky | solution.py:47
  309.1 5.3 select_select_fusion.1
  315.4 22.0 %while.8 = (s32[]{:T(128)}, f32[2,768,768]{2,1,0:T(8,128)}, s32[6,2]{0,1:T(2,128)S(1)}, f32[6,2,128,128]{3,2,0,1:T(8,128)}, s32[]{:T(128)}) while((s32[]{:T(128)}, f32[2,768,768]{2,1,0:T(8,128)}, s32[6,2]{0,1:T(2,128)S(1)}, f32[6,2,128,128]{3,2,0,1:T(8,128)}, s32[]{:T(128)}) %tuple.92), condition=%wide.while_cond.1, body=%wide.while_body.1.sunk | while | flops 2 | bytes 263777 | solution.py:56
  316.1 3.0 bitcast_dynamic-update-slice_fusion.4
  319.8 3.0 bitcast_dynamic-update-slice_fusion.4
  323.5 3.0 bitcast_dynamic-update-slice_fusion.4
  327.1 3.0 bitcast_dynamic-update-slice_fusion.4
  330.8 3.0 bitcast_dynamic-update-slice_fusion.4
  337.5 119.5 %custom-call.69 = f32[2,6,128,128]{2,3,1,0:T(8,128)} custom-call(f32[2,6,128,128]{3,2,1,0:T(8,128)} %bitcast.493), custom_call_target="InvertDiagBlocksLowerTriangular" | custom-call | tf_op jit(solution)/shard_map/triangular_solve/custom-call.12 | solution.py:56
  487.4 4.6 fusion.3
  503.8 3.2 collective-permute-start.2
  512.5 3.3 collective-permute-start.4
  522.3 12.0 %psum.14 = f32[2,768]{1,0:T(2,128)S(1)} all-reduce(f32[2,768]{1,0:T(2,128)S(1)} %fusion.118), channel_id=1, replica_groups=mesh['samp'=32,'slab'=4] {'slab'}, use_global_device_ids=true, to_apply=%region_15.19 | all-reduce | flops 1536 | bytes 12288 | tf_op jit(solution)/shard_map/psum | solution.py:69
  534.9 4.5 multiply_add_fusion
  539.4 6.1 copy.134
  545.5 4.4 fusion
  552.0 23.5 %custom-call.70 = f32[2,128,128]{2,1,0:T(8,128)S(1)} custom-call(f32[2,128,128]{2,1,0:T(8,128)S(1)} %cholesky.685), custom_call_target="Cholesky" | custom-call | tf_op jit(solution)/shard_map/jit(cholesky)/cholesky | solution.py:47
  577.9 19.7 %custom-call.71 = f32[2,1,128,128]{2,3,1,0:T(8,128)S(1)} custom-call(f32[2,1,128,128]{3,2,1,0:T(8,128)S(1)} %select_bitcast_fusion.4), custom_call_target="InvertDiagBlocksLowerTriangular" | custom-call | tf_op jit(solution)/shard_map/jit(cholesky)/cholesky | solution.py:47
  603.1 23.9 %custom-call.72 = f32[2,128,128]{2,1,0:T(8,128)S(1)} custom-call(f32[2,128,128]{2,1,0:T(8,128)S(1)} %cholesky.689), custom_call_target="Cholesky" | custom-call | tf_op jit(solution)/shard_map/jit(cholesky)/cholesky | solution.py:47
  627.7 19.7 %custom-call.73 = f32[2,1,128,128]{2,3,1,0:T(8,128)S(1)} custom-call(f32[2,1,128,128]{3,2,1,0:T(8,128)S(1)} %get-tuple-element.86), custom_call_target="InvertDiagBlocksLowerTriangular" | custom-call | tf_op jit(solution)/shard_map/jit(cholesky)/cholesky | solution.py:47
  653.2 23.5 %custom-call.74 = f32[2,128,128]{2,1,0:T(8,128)S(1)} custom-call(f32[2,128,128]{2,1,0:T(8,128)S(1)} %cholesky.694), custom_call_target="Cholesky" | custom-call | tf_op jit(solution)/shard_map/jit(cholesky)/cholesky | solution.py:47
  677.4 20.6 %custom-call.75 = f32[2,1,128,128]{2,3,1,0:T(8,128)S(1)} custom-call(f32[2,1,128,128]{3,2,1,0:T(8,128)} %get-tuple-element.84), custom_call_target="InvertDiagBlocksLowerTriangular" | custom-call | tf_op jit(solution)/shard_map/jit(cholesky)/cholesky | solution.py:47
  703.7 24.9 %custom-call.76 = f32[2,128,128]{2,1,0:T(8,128)} custom-call(f32[2,128,128]{2,1,0:T(8,128)} %cholesky.699), custom_call_target="Cholesky" | custom-call | tf_op jit(solution)/shard_map/jit(cholesky)/cholesky | solution.py:47
  730.3 21.1 %custom-call.77 = f32[2,1,128,128]{2,3,1,0:T(8,128)} custom-call(f32[2,1,128,128]{3,2,1,0:T(8,128)} %get-tuple-element.82), custom_call_target="InvertDiagBlocksLowerTriangular" | custom-call | tf_op jit(solution)/shard_map/jit(cholesky)/cholesky | solution.py:47
  756.5 24.5 %custom-call.78 = f32[2,128,128]{2,1,0:T(8,128)S(1)} custom-call(f32[2,128,128]{2,1,0:T(8,128)} %cholesky.704), custom_call_target="Cholesky" | custom-call | tf_op jit(solution)/shard_map/jit(cholesky)/cholesky | solution.py:47
  781.8 21.1 %custom-call.79 = f32[2,1,128,128]{2,3,1,0:T(8,128)} custom-call(f32[2,1,128,128]{3,2,1,0:T(8,128)} %get-tuple-element.80), custom_call_target="InvertDiagBlocksLowerTriangular" | custom-call | tf_op jit(solution)/shard_map/jit(cholesky)/cholesky | solution.py:47
  806.9 23.5 %custom-call.80 = f32[2,128,128]{2,1,0:T(8,128)S(1)} custom-call(f32[2,128,128]{2,1,0:T(8,128)S(1)} %convolution_subtract_fusion.8), custom_call_target="Cholesky" | custom-call | tf_op jit(solution)/shard_map/jit(cholesky)/cholesky | solution.py:47
  832.9 5.3 select_select_fusion
  839.3 21.4 %while.9 = (s32[]{:T(128)}, f32[2,768,768]{2,1,0:T(8,128)}, s32[6,2]{0,1:T(2,128)S(1)}, f32[6,2,128,128]{3,2,0,1:T(8,128)}, s32[]{:T(128)}) while((s32[]{:T(128)}, f32[2,768,768]{2,1,0:T(8,128)}, s32[6,2]{0,1:T(2,128)S(1)}, f32[6,2,128,128]{3,2,0,1:T(8,128)}, s32[]{:T(128)}) %tuple.98), condition=%wide.while_cond.1.clone, body=%wide.while_body.1.clone.sunk | while | flops 2 | bytes 263777 | solution.py:56
  860.7 119.7 %custom-call.82 = f32[2,6,128,128]{2,3,1,0:T(8,128)} custom-call(f32[2,6,128,128]{3,2,1,0:T(8,128)} %bitcast.492), custom_call_target="InvertDiagBlocksLowerTriangular" | custom-call | tf_op jit(solution)/shard_map/triangular_solve/custom-call.12 | solution.py:56
  1009.4 3.6 fusion.2
  1013.7 25.2 %all_gather.3 = f32[2,49152]{1,0:T(2,128)S(1)} all-gather(f32[2,1536]{1,0:T(2,128)S(1)} %pad_maximum_fusion), channel_id=1, replica_groups=mesh['samp'=32,'slab'=4] {'samp'}, dimensions={1}, use_global_device_ids=true | all-gather | bytes 405504 | tf_op jit(solution)/shard_map/all_gather | solution.py:82
  1041.8 3.6 all-to-all-start
  1079.5 11.1 %all-reduce.2 = (f32[2,768]{1,0:T(2,128)S(1)}, f32[128,4]{0,1:T(4,128)S(1)}) all-reduce(f32[2,768]{1,0:T(2,128)} %fusion.119, f32[128,4]{0,1:T(4,128)S(1)} %fusion.13), channel_id=1, replica_groups=mesh['samp'=32,'slab'=4] {'slab'}, use_global_device_ids=true, to_apply=%region_18.22 | all-reduce | flops 2048 | bytes 16384 | tf_op jit(solution)/shard_map/psum | solution.py:69
  (359 shorter events, 227.8 us)
Async XLA Ops:
  0.6 1078.0 %copy-start = (bf16[128,12288]{1,0:T(8,128)(2,1)S(1)}, bf16[128,12288]{1,0:T(8,128)(2,1)}, u32[]{:S(2)}) copy-start(bf16[128,12288]{1,0:T(8,128)(2,1)} %param.18) | copy-start | bytes 9437188
  0.6 10.0 copy-start.30
  0.7 10.1 copy-start.38
  10.7 11.1 %copy-start.14 = (f32[2,768]{1,0:T(2,128)}, f32[2,768]{1,0:T(2,128)S(1)}, u32[]{:S(2)}) copy-start(f32[2,768]{1,0:T(2,128)S(1)} %fusion.132) | copy-start | bytes 18436
  11.4 4.3 copy-start.24
  26.2 2.1 copy-start.3
  51.8 27.6 %copy-start.8 = (f32[2,128,128]{2,1,0:T(8,128)}, f32[2,128,128]{2,1,0:T(8,128)S(1)}, u32[]{:S(2)}) copy-start(f32[2,128,128]{2,1,0:T(8,128)S(1)} %custom-call.57) | copy-start | bytes 393220
  103.1 71.2 %copy-start.10 = (f32[2,128,128]{2,1,0:T(8,128)}, f32[2,128,128]{2,1,0:T(8,128)S(1)}, u32[]{:S(2)}) copy-start(f32[2,128,128]{2,1,0:T(8,128)S(1)} %custom-call.59) | copy-start | bytes 393220
  152.8 21.5 %copy-start.12 = (f32[2,128,128]{2,1,0:T(8,128)}, f32[2,128,128]{2,1,0:T(8,128)S(1)}, u32[]{:S(2)}) copy-start(f32[2,128,128]{2,1,0:T(8,128)S(1)} %custom-call.61) | copy-start | bytes 393220
  309.1 5.3 copy-start.41
  309.1 147.9 %copy-start.31 = (s32[2]{0:T(128)S(1)}, s32[2]{0:T(128)}, u32[]{:S(2)}) copy-start(s32[2]{0:T(128)} %param.15) | copy-start | bytes 28
  309.1 147.9 %copy-start.34 = (f32[2,768,1]{1,0,2:T(2,128)S(1)}, f32[2,768,1]{1,0,2:T(2,128)}, u32[]{:S(2)}) copy-start(f32[2,768,1]{1,0,2:T(2,128)} %reshape_squeeze.13) | copy-start | bytes 18436
  314.4 157.1 %copy-start.39 = (f32[4]{0:T(128)S(1)}, f32[4]{0:T(128)}, u32[]{:S(2)}) copy-start(f32[4]{0:T(128)} %param.17) | copy-start | bytes 52
  314.4 158.6 %copy-start.35 = (f32[2,1,1536]{2,1,0:T(1,128)S(1)}, f32[2,1,1536]{2,1,0:T(1,128)}, u32[]{:S(2)}) copy-start(f32[2,1,1536]{2,1,0:T(1,128)} %param.14) | copy-start | bytes 36868
  314.4 173.0 %copy-start.15 = (f32[2,768]{1,0:T(2,128)S(1)}, f32[2,768]{1,0:T(2,128)}, u32[]{:S(2)}) copy-start(f32[2,768]{1,0:T(2,128)} %copy-done.14) | copy-start | bytes 18436
  337.5 154.6 %copy-start.17 = (s32[6,2]{0,1:T(2,128)}, s32[6,2]{0,1:T(2,128)S(1)}, u32[]{:S(2)}) copy-start(s32[6,2]{0,1:T(2,128)S(1)} %get-tuple-element.228) | copy-start | bytes 148
  457.0 30.3 %copy-start.27 = (f32[2,768,1]{1,0,2:T(2,128)}, f32[2,768,1]{1,0,2:T(2,128)S(1)}, u32[]{:S(2)}) copy-start(f32[2,768,1]{1,0,2:T(2,128)S(1)} %fusion.130) | copy-start | bytes 18436
  457.1 15.9 %copy-start.36 = (f32[2,128,1]{1,0,2:T(2,128)}, f32[2,128,1]{1,0,2:T(2,128)S(1)}, u32[]{:S(2)}) copy-start(f32[2,128,1]{1,0,2:T(2,128)S(1)} %slice.368) | copy-start | bytes 3076
  463.0 29.1 %copy-start.25 = (f32[2,768]{1,0:T(2,128)S(1)}, f32[2,768]{1,0:T(2,128)}, u32[]{:S(2)}) copy-start(f32[2,768]{1,0:T(2,128)} %copy-done.24) | copy-start | bytes 18436
  463.0 29.1 %copy-start.26 = (f32[2,768]{1,0:T(2,128)S(1)}, f32[2,768]{1,0:T(2,128)}, u32[]{:S(2)}) copy-start(f32[2,768]{1,0:T(2,128)} %reshape_squeeze.15) | copy-start | bytes 18436
  463.0 31.9 %copy-start.29 = (f32[1536]{0:T(1024)S(1)}, f32[1536]{0:T(1024)}, u32[]{:S(2)}) copy-start(f32[1536]{0:T(1024)} %get-tuple-element.97) | copy-start | bytes 18436
  463.0 32.5 %copy-start.40 = (u32[128]{0:T(128)S(1)}, u32[128]{0:T(128)}, u32[]{:S(2)}) copy-start(u32[128]{0:T(128)} %constant.263) | copy-start | bytes 1540
  494.9 1.3 collective-permute-start
  494.9 44.5 %copy-start.19 = (f32[2,768]{1,0:T(2,128)}, f32[2,768]{1,0:T(2,128)S(1)}, u32[]{:S(2)}) copy-start(f32[2,768]{1,0:T(2,128)S(1)} %mul.160) | copy-start | bytes 18436
  498.2 3.6 collective-permute-start.1
  503.8 5.1 collective-permute-start.2
  508.9 3.6 collective-permute-start.3
  512.5 5.1 collective-permute-start.4
  534.3 5.1 copy-start.21
  575.4 27.6 %copy-start.9 = (f32[2,128,128]{2,1,0:T(8,128)}, f32[2,128,128]{2,1,0:T(8,128)S(1)}, u32[]{:S(2)}) copy-start(f32[2,128,128]{2,1,0:T(8,128)S(1)} %custom-call.70) | copy-start | bytes 393220
  626.9 71.1 %copy-start.11 = (f32[2,128,128]{2,1,0:T(8,128)}, f32[2,128,128]{2,1,0:T(8,128)S(1)}, u32[]{:S(2)}) copy-start(f32[2,128,128]{2,1,0:T(8,128)S(1)} %custom-call.72) | copy-start | bytes 393220
  676.6 21.4 %copy-start.13 = (f32[2,128,128]{2,1,0:T(8,128)}, f32[2,128,128]{2,1,0:T(8,128)S(1)}, u32[]{:S(2)}) copy-start(f32[2,128,128]{2,1,0:T(8,128)S(1)} %custom-call.74) | copy-start | bytes 393220
  832.9 6.4 copy-start.18
  832.9 147.5 %copy-start.37 = (f32[2,128,1]{1,0,2:T(2,128)S(1)}, f32[2,128,1]{1,0,2:T(2,128)}, u32[]{:S(2)}) copy-start(f32[2,128,1]{1,0,2:T(2,128)} %copy-done.36) | copy-start | bytes 3076
  832.9 150.0 %copy-start.28 = (f32[2,768,1]{1,0,2:T(2,128)S(1)}, f32[2,768,1]{1,0,2:T(2,128)}, u32[]{:S(2)}) copy-start(f32[2,768,1]{1,0,2:T(2,128)} %copy-done.27) | copy-start | bytes 18436
  838.3 156.8 %copy-start.32 = (s32[2]{0:T(128)S(1)}, s32[2]{0:T(128)}, u32[]{:S(2)}) copy-start(s32[2]{0:T(128)} %param.15) | copy-start | bytes 28
  838.3 156.8 %copy-start.33 = (f32[2,768,1]{1,0,2:T(2,128)S(1)}, f32[2,768,1]{1,0,2:T(2,128)}, u32[]{:S(2)}) copy-start(f32[2,768,1]{1,0,2:T(2,128)} %mul.175) | copy-start | bytes 18436
  838.3 171.2 %copy-start.16 = (f32[2,768]{1,0:T(2,128)S(1)}, f32[2,768]{1,0:T(2,128)}, u32[]{:S(2)}) copy-start(f32[2,768]{1,0:T(2,128)} %copy-done.14) | copy-start | bytes 18436
  980.4 29.0 %copy-start.1 = (bf16[1,2,768,768]{2,3,1,0:T(8,128)(2,1)S(1)}, bf16[1,2,768,768]{2,3,1,0:T(8,128)(2,1)}, u32[]{:S(2)}) copy-start(bf16[1,2,768,768]{2,3,1,0:T(8,128)(2,1)} %copy.120) | copy-start | bytes 7077892
  986.5 26.6 %copy-start.23 = (f32[1,1,2,768]{3,1,2,0:T(1,128)S(1)}, f32[1,1,2,768]{3,1,2,0:T(1,128)}, u32[]{:S(2)}) copy-start(f32[1,1,2,768]{3,1,2,0:T(1,128)} %copy.275) | copy-start | bytes 18436
  1013.1 77.6 %copy-start.20 = (f32[2,768]{1,0:T(2,128)S(1)}, f32[2,768]{1,0:T(2,128)}, u32[]{:S(2)}) copy-start(f32[2,768]{1,0:T(2,128)} %copy-done.19) | copy-start | bytes 18436
  1041.8 34.1 %all-to-all-start = ((f32[1,2,32,4,384]{4,2,1,0,3:T(8,128)}), f32[1,2,32,4,384]{4,2,1,0,3:T(8,128)S(1)}, u32[]{:S(2)}, u32[]{:S(2)}) async-start(f32[1,2,32,4,384]{4,2,1,0,3:T(8,128)} %copy.147), calls=%async_computation | async-start | bytes 786432 | tf_op jit(solution)/shard_map/all_to_all | solution.py:84
  1048.9 1.2 collective-permute-start.5
  1052.1 3.6 collective-permute-start.6
  1057.7 5.1 collective-permute-start.7
  1062.7 3.6 collective-permute-start.8
  1066.3 5.1 collective-permute-start.9
  1076.0 14.7 %copy-start.22 = (f32[2,768]{1,0:T(2,128)S(1)}, f32[2,768]{1,0:T(2,128)}, u32[]{:S(2)}) copy-start(f32[2,768]{1,0:T(2,128)} %copy-done.21) | copy-start | bytes 18436
  (5 other events, 5.4 us)
